TPU v7x, 32 devices: a whole 2x2x4 slice. The times are simulated.
32 devices in a mesh: row: 4 (over y, x), col: 8 (over z, core).
Axes of the slice: x: 2, y: 2, z: 4, core: 2. Of those that a mesh axis runs over, the one named last changes fastest.
Arguments:
- tokens: bfloat16 [294912, 1024], P(('row', 'col')), may hold values from -6 to 6
- router_weight: bfloat16 [1024], P(('row', 'col')), may hold values from -0.1875 to 0.1875
- norm_first: bfloat16 [1024], P(('row', 'col')), may hold values from 0.099609375 to 1.8984375
- qkv_weight: bfloat16 [1024, 3072], P('row', 'col'), may hold values from -0.1875 to 0.1875
- out_weight: bfloat16 [1024, 1024], P('col', 'row'), may hold values from -0.75 to 0.75
- norm_second: bfloat16 [1024], P(('row', 'col')), may hold values from 0.099609375 to 1.8984375
- up_weight: bfloat16 [1024, 4096], P('row', 'col'), may hold values from -0.1875 to 0.1875
- down_weight: bfloat16 [4096, 1024], P('col', 'row'), may hold values from -0.09375 to 0.09375
- route_index: int32 [288, 128], P(('row', 'col')), may hold values from 0 to 1023, as said below
- out_cotangent: bfloat16 [294912, 1024], P(('row', 'col')), may hold values from -6 to 6
Outputs:
- output: bfloat16 [294912, 1024], P(('row', 'col'))
- input_grad: float32 [294912, 1024], P(('row', 'col'))
- router_grad: float32 [1024], P(('row', 'col'))
- norm_first_grad: float32 [1024], P(('row', 'col'))
- qkv_grad: float32 [1024, 3072], P('row', 'col')
- out_grad: float32 [1024, 1024], P('col', 'row')
- norm_second_grad: float32 [1024], P(('row', 'col'))
- up_grad: float32 [1024, 4096], P('row', 'col')
- down_grad: float32 [4096, 1024], P('col', 'row')
Inputs may be any that keep to these rules, and one draw needn't show every extreme that they name: `route_index`: each row lists 128 distinct positions of one sequence in increasing order; the first is 0 and the last 1023.
All inputs are finite; a program needn't handle non-finite values.
Results may differ from a plain program's by a relative error of at most 0.019.
Values may be sent and summed in bfloat16 or wider, within the bound.
No kernel may reach another device: no remote copies, remote signals or barrier semaphores. Data moves between devices by JAX's collectives and lax.ppermute only.
A program may use at most 320 MiB of HBM per device.

v0:
```python
import jax
import jax.numpy as jnp
from jax import lax
from jax.sharding import PartitionSpec as P

HEADS = 16
HD = 64
epsilon = 1e-06


def local(
    tokens,
    router_weight,
    norm_first,
    qkv_weight,
    out_weight,
    norm_second,
    up_weight,
    down_weight,
    route_index,
    out_cotangent,
):
    seq_local, routed = route_index.shape
    seq_length = tokens.shape[0] // seq_local
    width = tokens.shape[1]
    starts = jnp.arange(seq_local, dtype=jnp.int32) * seq_length
    token_rows = (route_index + starts[:, None]).reshape(-1)
    row_count = token_rows.shape[0]
    col_pieces = (
        lax.all_gather(qkv_weight, "col", axis=1, tiled=True),
        lax.all_gather(out_weight, "col", axis=0, tiled=True),
        lax.all_gather(up_weight, "col", axis=1, tiled=True),
        lax.all_gather(down_weight, "col", axis=0, tiled=True),
        lax.all_gather(norm_first, "col", axis=0, tiled=True),
        lax.all_gather(norm_second, "col", axis=0, tiled=True),
        lax.all_gather(router_weight, "col", axis=0, tiled=True),
    )
    gathered = (
        lax.all_gather(col_pieces[0], "row", axis=0, tiled=True),
        lax.all_gather(col_pieces[1], "row", axis=1, tiled=True),
        lax.all_gather(col_pieces[2], "row", axis=0, tiled=True),
        lax.all_gather(col_pieces[3], "row", axis=1, tiled=True),
        lax.all_gather(col_pieces[4], "row", axis=0, tiled=True),
        lax.all_gather(col_pieces[5], "row", axis=0, tiled=True),
        lax.all_gather(col_pieces[6], "row", axis=0, tiled=True),
    )
    w_qkv, w_out, w_up, w_down, first_full, second_full, router_full = gathered
    first_gain = first_full.astype(jnp.float32)
    second_gain = second_full.astype(jnp.float32)
    router_vec = router_full.astype(jnp.float32)
    picked_full = tokens[token_rows]
    h_full = picked_full.astype(jnp.float32)
    gate_value = jax.nn.sigmoid(
        jnp.dot(picked_full, router_full, preferred_element_type=jnp.float32)
    )
    inverse_first = lax.rsqrt(jnp.mean(h_full * h_full, axis=-1, keepdims=True) + epsilon)
    normed = (h_full * inverse_first * first_gain).astype(jnp.bfloat16)
    projected = jnp.dot(normed, w_qkv, preferred_element_type=jnp.float32).astype(jnp.bfloat16)
    heads_qkv = projected.reshape(seq_local, routed, HEADS, 3, HD)
    queries = heads_qkv[:, :, :, 0]
    key_rows = heads_qkv[:, :, :, 1]
    values = heads_qkv[:, :, :, 2]
    scaling = HD ** (-0.5)
    places = jnp.arange(routed, dtype=jnp.int32)
    causal = places[:, None] >= places[None, :]
    scores = (
        jnp.einsum("sqhe,skhe->shqk", queries, key_rows, preferred_element_type=jnp.float32)
        * scaling
    )
    scores = jnp.where(causal, scores, -1e30)
    highest = jnp.max(scores, axis=-1, keepdims=True)
    expanded = jnp.exp(scores - highest)
    totals = jnp.sum(expanded, axis=-1, keepdims=True)
    attn_probs = (expanded / totals).astype(jnp.bfloat16)
    log_total = highest + jnp.log(totals)
    mixed = jnp.einsum("shqk,skhe->sqhe", attn_probs, values, preferred_element_type=jnp.float32)
    context = mixed.reshape(row_count, width).astype(jnp.bfloat16)
    attn_out = jnp.dot(context, w_out, preferred_element_type=jnp.float32)
    middle = h_full + attn_out
    inverse_mid = lax.rsqrt(jnp.mean(middle * middle, axis=-1, keepdims=True) + epsilon)
    normed_mid = (middle * inverse_mid * second_gain).astype(jnp.bfloat16)
    pre_act = jnp.dot(normed_mid, w_up, preferred_element_type=jnp.float32)
    activated, gelu_back = jax.vjp(jax.nn.gelu, pre_act)
    hidden = activated.astype(jnp.bfloat16)
    mlp_out = jnp.dot(hidden, w_down, preferred_element_type=jnp.float32)
    branch = attn_out + mlp_out
    output = (
        tokens.astype(jnp.float32)
        .at[token_rows]
        .add(gate_value[:, None] * branch)
        .astype(jnp.bfloat16)
    )
    back_pieces = (
        lax.all_gather(qkv_weight, "col", axis=1, tiled=True),
        lax.all_gather(out_weight, "col", axis=0, tiled=True),
        lax.all_gather(up_weight, "col", axis=1, tiled=True),
        lax.all_gather(down_weight, "col", axis=0, tiled=True),
    )
    w_qkv, w_out, w_up, w_down = (
        lax.all_gather(back_pieces[0], "row", axis=0, tiled=True),
        lax.all_gather(back_pieces[1], "row", axis=1, tiled=True),
        lax.all_gather(back_pieces[2], "row", axis=0, tiled=True),
        lax.all_gather(back_pieces[3], "row", axis=1, tiled=True),
    )
    grad_out = out_cotangent.astype(jnp.float32)
    grad_rows = grad_out[token_rows]
    gate_grad = jnp.sum(grad_rows * branch, axis=-1)
    grad_branch = gate_value[:, None] * grad_rows
    grad_mlp = grad_branch.astype(jnp.bfloat16)
    grad_hidden = jnp.dot(grad_mlp, w_down.T, preferred_element_type=jnp.float32)
    down_part = jnp.dot(hidden.T, grad_mlp, preferred_element_type=jnp.float32)
    grad_pre = gelu_back(grad_hidden)[0].astype(jnp.bfloat16)
    up_part = jnp.dot(normed_mid.T, grad_pre, preferred_element_type=jnp.float32)
    grad_normed_mid = jnp.dot(grad_pre, w_up.T, preferred_element_type=jnp.float32)
    second_part = jnp.sum(grad_normed_mid * middle * inverse_mid, axis=0)
    grad_scaled_mid = grad_normed_mid * second_gain
    mid_sum = jnp.sum(grad_scaled_mid * middle, axis=-1, keepdims=True)
    grad_middle = inverse_mid * grad_scaled_mid - middle * inverse_mid**3 * mid_sum / width
    grad_attn = (grad_branch + grad_middle).astype(jnp.bfloat16)
    grad_context = jnp.dot(grad_attn, w_out.T, preferred_element_type=jnp.float32).astype(
        jnp.bfloat16
    )
    out_part = jnp.dot(context.T, grad_attn, preferred_element_type=jnp.float32)
    grad_heads = grad_context.reshape(seq_local, routed, HEADS, HD)
    again = (
        jnp.einsum("sqhe,skhe->shqk", queries, key_rows, preferred_element_type=jnp.float32)
        * scaling
    )
    again = jnp.where(causal, again, -1e30)
    probs_exact = jnp.exp(again - log_total)
    grad_probs = jnp.einsum(
        "sqhe,skhe->shqk", grad_heads, values, preferred_element_type=jnp.float32
    )
    inner_sum = jnp.sum(grad_probs * probs_exact, axis=-1, keepdims=True)
    grad_scores = (probs_exact * (grad_probs - inner_sum)).astype(jnp.bfloat16)
    grad_query = (
        jnp.einsum("shqk,skhe->sqhe", grad_scores, key_rows, preferred_element_type=jnp.float32)
        * scaling
    )
    grad_key = (
        jnp.einsum("shqk,sqhe->skhe", grad_scores, queries, preferred_element_type=jnp.float32)
        * scaling
    )
    grad_value = jnp.einsum(
        "shqk,sqhe->skhe", attn_probs, grad_heads, preferred_element_type=jnp.float32
    )
    grad_projected = (
        jnp.stack([grad_query, grad_key, grad_value], axis=3)
        .reshape(row_count, 3 * width)
        .astype(jnp.bfloat16)
    )
    qkv_part = jnp.dot(normed.T, grad_projected, preferred_element_type=jnp.float32)
    grad_normed = jnp.dot(grad_projected, w_qkv.T, preferred_element_type=jnp.float32)
    first_part = jnp.sum(grad_normed * h_full * inverse_first, axis=0)
    grad_scaled_first = grad_normed * first_gain
    first_sum = jnp.sum(grad_scaled_first * h_full, axis=-1, keepdims=True)
    grad_norm_in = inverse_first * grad_scaled_first - h_full * inverse_first**3 * first_sum / width
    grad_logit = gate_grad * gate_value * (1.0 - gate_value)
    router_part = jnp.sum(grad_logit[:, None] * h_full, axis=0)
    grad_picked = grad_middle + grad_norm_in + grad_logit[:, None] * router_vec
    input_grad = grad_out.at[token_rows].add(grad_picked)
    all_pieces = (
        lax.psum_scatter(
            qkv_part.astype(jnp.bfloat16), "row", scatter_dimension=0, tiled=True
        ).astype(jnp.float32),
        lax.psum_scatter(
            out_part.astype(jnp.bfloat16), "row", scatter_dimension=1, tiled=True
        ).astype(jnp.float32),
        lax.psum_scatter(
            up_part.astype(jnp.bfloat16), "row", scatter_dimension=0, tiled=True
        ).astype(jnp.float32),
        lax.psum_scatter(
            down_part.astype(jnp.bfloat16), "row", scatter_dimension=1, tiled=True
        ).astype(jnp.float32),
        lax.psum_scatter(
            first_part.astype(jnp.bfloat16), "row", scatter_dimension=0, tiled=True
        ).astype(jnp.float32),
        lax.psum_scatter(
            second_part.astype(jnp.bfloat16), "row", scatter_dimension=0, tiled=True
        ).astype(jnp.float32),
        lax.psum_scatter(
            router_part.astype(jnp.bfloat16), "row", scatter_dimension=0, tiled=True
        ).astype(jnp.float32),
    )
    summed = (
        lax.psum_scatter(
            all_pieces[0].astype(jnp.bfloat16), "col", scatter_dimension=1, tiled=True
        ).astype(jnp.float32),
        lax.psum_scatter(
            all_pieces[1].astype(jnp.bfloat16), "col", scatter_dimension=0, tiled=True
        ).astype(jnp.float32),
        lax.psum_scatter(
            all_pieces[2].astype(jnp.bfloat16), "col", scatter_dimension=1, tiled=True
        ).astype(jnp.float32),
        lax.psum_scatter(
            all_pieces[3].astype(jnp.bfloat16), "col", scatter_dimension=0, tiled=True
        ).astype(jnp.float32),
        lax.psum_scatter(
            all_pieces[4].astype(jnp.bfloat16), "col", scatter_dimension=0, tiled=True
        ).astype(jnp.float32),
        lax.psum_scatter(
            all_pieces[5].astype(jnp.bfloat16), "col", scatter_dimension=0, tiled=True
        ).astype(jnp.float32),
        lax.psum_scatter(
            all_pieces[6].astype(jnp.bfloat16), "col", scatter_dimension=0, tiled=True
        ).astype(jnp.float32),
    )
    qkv_grad, out_grad, up_grad, down_grad, norm_first_grad, norm_second_grad, router_grad = summed
    return (
        output,
        input_grad,
        router_grad,
        norm_first_grad,
        qkv_grad,
        out_grad,
        norm_second_grad,
        up_grad,
        down_grad,
    )


def solution(mesh):
    placed = (
        P(("row", "col"), None),
        P(("row", "col")),
        P(("row", "col")),
        P("row", "col"),
        P("col", "row"),
        P(("row", "col")),
        P("row", "col"),
        P("col", "row"),
        P(("row", "col"), None),
        P(("row", "col"), None),
    )
    return jax.shard_map(
        local,
        mesh=mesh,
        in_specs=placed,
        out_specs=(
            P(("row", "col"), None),
            P(("row", "col"), None),
            P(("row", "col")),
            P(("row", "col")),
            P("row", "col"),
            P("col", "row"),
            P(("row", "col")),
            P("row", "col"),
            P("col", "row"),
        ),
        check_vma=False,
    )
```

profile of v0, /device:TPU:0, one launch (start us, length us, event | category | flops | bytes accessed | tf_op | source)
XLA Modules:
  0.0 964.3 jit_solution(17025223967984651840)
XLA Ops:
  9.5 28.1 %all-gather.11.cloned.1.call-done = bf16[256,3072]{1,0:T(8,128)(2,1)} async-done(((bf16[256,384]{1,0:T(8,128)(2,1)}), bf16[256,3072]{1,0:T(8,128)(2,1)}) %all-gather.11.cloned.1.call-update) | async-done | bytes 1572880 | tf_op jit(solution)/shard_map/all_gather | solution.py:30
  37.7 16.9 %all_gather.56 = bf16[1024,256]{1,0:T(8,128)(2,1)} all-gather(bf16[128,256]{1,0:T(8,128)(2,1)} %param.14), channel_id=1, replica_groups=mesh['row'=4,'col'=8] {'col'}, dimensions={0}, use_global_device_ids=true | all-gather | bytes 589824 | tf_op jit(solution)/shard_map/all_gather | solution.py:31
  54.7 14.2 %all-gather.17.cloned.1.call-done = bf16[256,4096]{1,0:T(8,128)(2,1)} async-done(((bf16[256,512]{1,0:T(8,128)(2,1)}), bf16[256,4096]{1,0:T(8,128)(2,1)}) %all-gather.17.cloned.1.call-update) | async-done | bytes 2097168 | tf_op jit(solution)/shard_map/all_gather | solution.py:32
  71.0 15.3 %all-reduce.10 = (bf16[256]{0:T(256)(128)(2,1)S(1)}, bf16[256]{0:T(256)(128)(2,1)S(1)}, bf16[256]{0:T(256)(128)(2,1)S(1)}) all-reduce(bf16[256]{0:T(256)(128)(2,1)S(1)} %dynamic-update-slice.1, bf16[256]{0:T(256)(128)(2,1)S(1)} %dynamic-update-slice.2, bf16[256]{0:T(256)(128)(2,1)S(1)} %dynamic-update-slice), channel_id=1, replica_groups=mesh['row'=4,'col'=8] {'col'}, use_global_device_ids=true, to_apply=%add.1 | all-reduce | flops 768 | bytes 3072
  86.3 7.9 all-gather.2
  94.2 8.0 all-gather.1
  102.9 16.6 %gather_fusion = bf16[1152,1024]{1,0:T(8,128)(2,1)} fusion(bf16[9216,1024]{1,0:T(8,128)(2,1)} %param.10, s32[2048]{0:T(1024)S(1)} %pad_clamp_fusion), kind=kCustom, calls=%fused_computation | custom fusion | bytes 4723200 | tf_op jit(solution)/shard_map/gather | solution.py:51
  119.5 3.0 copy.57
  122.5 21.7 %convert_element_type.133 = f32[9216,1024]{1,0:T(8,128)} convert(bf16[9216,1024]{1,0:T(8,128)(2,1)} %param.19) | non-fusion elementwise | flops 9437184 | bytes 56623104 | tf_op jit(solution)/shard_map/convert_element_type | solution.py:105
  144.2 18.3 %gather_fusion.1 = f32[1152,1024]{1,0:T(8,128)} fusion(f32[9216,1024]{1,0:T(8,128)} %convert_element_type.133, s32[2048]{0:T(1024)S(1)} %pad_clamp_fusion), kind=kCustom, calls=%fused_computation.1 | custom fusion | bytes 9441792 | tf_op jit(solution)/shard_map/gather | solution.py:106
  162.6 6.1 copy.65
  168.7 6.7 all-gather
  175.4 2.4 convolution_reduce_fusion
  179.3 12.8 %convolution_convert_fusion = bf16[1152,3072]{1,0:T(8,128)(2,1)} fusion(bf16[1024,3072]{1,0:T(8,128)(2,1)} %all-gather.13.cloned.1.call-done, bf16[1152,1024]{0,1:T(8,128)(2,1)S(1)} %copy.57, f32[1024]{0:T(1024)S(1)} %bitcast.115, f32[1152]{0:T(1024)S(1)} %get-tuple-element.32), kind=kOutput, calls=%fused_computation.21 | convolution fusion | flops 7256014848 | bytes 15737344 | tf_op jit(solution)/shard_map/dot_general | solution.py:58
  192.1 30.3 %reshape.178 = bf16[9,128,16,3,64]{4,3,2,1,0:T(4,128)(2,1)} reshape(bf16[1152,3072]{1,0:T(8,128)(2,1)} %convolution_convert_fusion) | data formatting | bytes 14155776 | tf_op jit(solution)/shard_map/reshape | solution.py:59
  222.4 35.7 %fusion.63 = (bf16[9,128,16,1,64]{4,3,2,1,0:T(2,128)(2,1)}, bf16[9,128,16,1,64]{4,3,2,1,0:T(2,128)(2,1)}, bf16[9,128,16,1,64]{4,3,2,1,0:T(2,128)(2,1)}) fusion(bf16[9,128,16,3,64]{4,3,2,1,0:T(4,128)(2,1)} %reshape.178), kind=kLoop, calls=%fused_computation.106 | loop fusion | bytes 14155776 | tf_op jit(solution)/shard_map/slice | solution.py:62
  258.1 18.9 %copy.91 = bf16[9,128,16,1,64]{1,4,2,0,3:T(8,128)(2,1)S(1)} copy(bf16[9,128,16,1,64]{4,3,2,1,0:T(2,128)(2,1)} %get-tuple-element.25) | data formatting | bytes 4718592
  277.0 20.0 %copy.92 = bf16[9,128,16,1,64]{1,4,2,0,3:T(8,128)(2,1)} copy(bf16[9,128,16,1,64]{4,3,2,1,0:T(2,128)(2,1)} %get-tuple-element.26) | data formatting | bytes 4718592
  297.0 20.3 %copy.93 = bf16[9,128,16,1,64]{1,4,2,0,3:T(8,128)(2,1)} copy(bf16[9,128,16,1,64]{4,3,2,1,0:T(2,128)(2,1)} %get-tuple-element.27) | data formatting | bytes 4718592
  317.2 4.5 fusion.15
  321.7 3.1 fusion.7
  325.4 2.8 divide_convert_fusion
  328.2 2.0 convert_bitcast_fusion.1
  330.3 4.4 copy.63
  334.7 10.3 %multiply_reduce_fusion.4 = (f32[1152]{0:T(1024)S(1)}, f32[1152,1024]{0,1:T(8,128)}, f32[1152,1024]{0,1:T(8,128)}) fusion(bf16[1152,1024]{0,1:T(8,128)(2,1)} %copy-done.4, bf16[1024,1024]{1,0:T(8,128)(2,1)} %all-gather.15.cloned.1.call-done, bf16[128,8,9,128]{3,2,1,0:T(8,128)(2,1)} %bitcast.106), kind=kOutput, calls=%fused_computation.58 | convolution fusion | flops 2420636672 | bytes 16257536 | tf_op jit(solution)/shard_map/dot_general | solution.py:78
  345.1 18.2 %fusion.62 = f32[1152,4096]{1,0:T(8,128)} fusion(bf16[1024,4096]{1,0:T(8,128)(2,1)} %all-gather.19.cloned.1.call-done, f32[1152,1024]{0,1:T(8,128)} %get-tuple-element.24, f32[1024]{0:T(1024)S(1)} %bitcast.110, f32[1152]{0:T(1024)S(1)} %get-tuple-element.34), kind=kOutput, calls=%fused_computation.105 | convolution fusion | flops 9667215360 | bytes 31990272 | tf_op jit(solution)/shard_map/dot_general | solution.py:82
  363.3 22.6 %all-gather.23.cloned.1.call-done = bf16[4096,1024]{1,0:T(8,128)(2,1)} async-done(((bf16[4096,256]{1,0:T(8,128)(2,1)}), bf16[4096,1024]{1,0:T(8,128)(2,1)}) %all-gather.23.cloned.1.call-update) | async-done | bytes 8388624 | tf_op jit(solution)/shard_map/all_gather | solution.py:42
  385.9 28.3 %fusion.6 = bf16[1152,4096]{1,0:T(8,128)(2,1)} fusion(f32[1152,4096]{1,0:T(8,128)} %fusion.62, bf16[4096,1024]{1,0:T(8,128)(2,1)} %all-gather.23.cloned.1.call-done, f32[1152,1024]{0,1:T(8,128)} %copy.65, f32[1152]{0:T(1024)S(1)} %add_divide_fusion), kind=kOutput, calls=%fused_computation.12 | convolution fusion | flops 9760407552 | bytes 41423360 | tf_op jit(solution)/shard_map/dot_general | solution.py:110
  414.1 19.3 %multiply_reduce_fusion.1 = (bf16[1024]{0:T(1024)(128)(2,1)}, f32[1152]{0:T(1024)S(1)}, f32[1152,1024]{0,1:T(8,128)}) fusion(f32[1152,1024]{0,1:T(8,128)} %get-tuple-element.24, f32[1152]{0:T(1024)S(1)} %get-tuple-element.34, f32[1024]{0:T(1024)S(1)} %bitcast.111, bf16[1152,4096]{1,0:T(8,128)(2,1)} %fusion.6, ...), kind=kOutput, calls=%fused_computation.50 | convolution fusion | flops 9670752256 | bytes 27278336 | tf_op jit(solution)/shard_map/dot_general | solution.py:114
  433.4 26.0 %multiply_reduce_fusion.2 = (f32[1152]{0:T(1024)}, f32[1152,1024]{0,1:T(8,128)}, bf16[1152,1024]{0,1:T(8,128)(2,1)}) fusion(f32[1152,1024]{0,1:T(8,128)} %copy.65, f32[1152]{0:T(1024)S(1)} %add_divide_fusion, f32[1152]{0:T(1024)S(1)} %get-tuple-element.10, f32[1152,1024]{0,1:T(8,128)} %get-tuple-element.24, f32[1152]{0:T(1024)S(1)} %get-tuple-element.33, ...), kind=kOutput, calls=%fused_computation.51 | convolution fusion | flops 9721478144 | bytes 53242368 | tf_op jit(solution)/shard_map/dot_general | solution.py:85
  459.4 7.2 fusion.53
  466.7 6.4 convolution_convert_fusion.3
  473.1 7.7 reshape.179
  480.8 6.9 copy.68
  487.7 7.9 convert_bitcast_fusion
  495.7 7.8 multiply_reduce_fusion
  503.4 11.7 %multiply_convert_fusion.1 = bf16[9,16,128,128]{2,3,1,0:T(8,128)(2,1)} fusion(f32[9,16,128,128]{2,3,1,0:T(8,128)} %get-tuple-element.42, f32[9,16,128,128]{2,3,1,0:T(8,128)} %copy-done, f32[9,16,128]{2,1,0:T(8,128)S(1)} %get-tuple-element.41, f32[9,16,128]{2,1,0:T(8,128)S(1)} %log_add_fusion, pred[128,128]{0,1:T(8,128)(4,1)S(1)} %iota_compare_fusion), kind=kLoop, calls=%fused_computation.22 | loop fusion | flops 14155776 | bytes 23756800 | tf_op jit(solution)/shard_map/convert_element_type | solution.py:135
  515.2 5.8 fusion.31
  521.0 1.5 fusion.30
  522.7 0.8 pad_maximum_fusion
  523.5 8.8 copy.73
  532.4 4.5 copy-done.8
  536.8 10.7 %fusion.12 = bf16[1024,3072]{1,0:T(8,128)(2,1)} fusion(bf16[384,8,9,128]{3,2,1,0:T(8,128)(2,1)S(1)} %bitcast.103, bf16[1152,1024]{0,1:T(8,128)(2,1)S(1)} %copy-done.5, f32[1024]{0:T(1024)S(1)} %bitcast.116, f32[1152]{0:T(1024)S(1)} %copy-done.18), kind=kOutput, calls=%fused_computation.36 | convolution fusion | flops 7255621632 | bytes 15737344 | tf_op jit(solution)/shard_map/dot_general | solution.py:152
  547.6 21.4 %convolution_convert_fusion.1 = bf16[4096,1024]{1,0:T(8,128)(2,1)} fusion(f32[1152,1024]{0,1:T(8,128)} %copy.65, f32[1152]{0:T(1024)S(1)} %add_divide_fusion, f32[1152,4096]{1,0:T(8,128)} %fusion.62), kind=kOutput, calls=%fused_computation.29 | convolution fusion | flops 9712697344 | bytes 31986176 | tf_op jit(solution)/shard_map/dot_general | solution.py:111
  569.1 18.3 %convolution_convert_fusion.2 = bf16[1024,4096]{1,0:T(8,128)(2,1)} fusion(bf16[1152,4096]{1,0:T(8,128)(2,1)} %fusion.6, f32[1152,1024]{0,1:T(8,128)} %get-tuple-element.24, f32[1024]{0:T(1024)S(1)} %bitcast.113, f32[1152]{0:T(1024)S(1)} %get-tuple-element.34), kind=kOutput, calls=%fused_computation.30 | convolution fusion | flops 9671409664 | bytes 22553088 | tf_op jit(solution)/shard_map/dot_general | solution.py:113
  588.0 29.9 %reduce-scatter.11.cloned.1.call-done = bf16[256,3072]{1,0:T(8,128)(2,1)} async-done(((bf16[1024,3072]{1,0:T(8,128)(2,1)}), bf16[256,3072]{1,0:T(8,128)(2,1)}) %reduce-scatter.11.cloned.1.call-update) | async-done | bytes 1572880 | tf_op jit(solution)/shard_map/reduce_scatter | solution.py:163
  618.0 2.6 copy.85
  620.6 86.9 %reduce-scatter.21.cloned.1.call-done = bf16[4096,256]{1,0:T(8,128)(2,1)} async-done(((bf16[4096,1024]{1,0:T(8,128)(2,1)}), bf16[4096,256]{1,0:T(8,128)(2,1)}) %reduce-scatter.21.cloned.1.call-update) | async-done | bytes 2097168 | tf_op jit(solution)/shard_map/reduce_scatter | solution.py:172
  707.7 21.3 %convert_element_type.120 = f32[9216,1024]{1,0:T(8,128)} convert(bf16[9216,1024]{1,0:T(8,128)(2,1)} %param.10) | non-fusion elementwise | flops 9437184 | bytes 56623104 | tf_op jit(solution)/shard_map/convert_element_type | solution.py:88
  730.9 6.1 copy.64
  737.0 60.6 %reduce-scatter.17.cloned.1.call-done = bf16[256,4096]{1,0:T(8,128)(2,1)} async-done(((bf16[1024,4096]{1,0:T(8,128)(2,1)}), bf16[256,4096]{1,0:T(8,128)(2,1)}) %reduce-scatter.17.cloned.1.call-update) | async-done | bytes 2097168 | tf_op jit(solution)/shard_map/reduce_scatter | solution.py:169
  797.7 15.1 %fusion.27 = (bf16[1024]{0:T(1024)(128)(2,1)S(1)}, f32[1152]{0:T(1024)S(1)}, bf16[1024]{0:T(1024)(128)(2,1)S(1)}, f32[1152,1024]{0,1:T(8,128)S(1)}) fusion(bf16[1152,1024]{0,1:T(8,128)(2,1)S(1)} %copy-done.5, f32[1152]{0:T(1024)S(1)} %copy-done.18, f32[1024]{0:T(1024)S(1)} %bitcast.117, f32[1152]{0:T(1024)S(1)} %subtract_multiply_fusion, ...), kind=kOutput, calls=%fused_computation.49 | convolution fusion | flops 7258371072 | bytes 20469248 | tf_op jit(solution)/shard_map/dot_general | solution.py:153
  812.8 6.7 fusion.23
  819.5 6.1 copy.76
  825.7 39.5 %scatter_fusion.1 = f32[9216,1024]{1,0:T(8,128)} fusion(f32[9216,1024]{1,0:T(8,128)} %convert_element_type.133, s32[1152]{0:T(1024)S(1)} %copy-done.11, f32[1152,1024]{1,0:T(8,128)} %copy.76), kind=kCustom, calls=%fused_computation.3 | custom fusion | flops 1179648 | bytes 14160384 | tf_op jit(solution)/shard_map/scatter-add | solution.py:161
  865.2 9.4 all-reduce.11
  874.8 39.4 %scatter_fusion = f32[9216,1024]{1,0:T(8,128)} fusion(f32[9216,1024]{1,0:T(8,128)} %convert_element_type.120, s32[1152]{0:T(1024)S(1)} %copy-done.11, f32[1152,1024]{1,0:T(8,128)} %copy.64), kind=kCustom, calls=%fused_computation.2 | custom fusion | flops 1179648 | bytes 14160384 | tf_op jit(solution)/shard_map/scatter-add | solution.py:90
  914.1 20.9 %convert_element_type.132 = bf16[9216,1024]{1,0:T(8,128)(2,1)} convert(f32[9216,1024]{1,0:T(8,128)} %scatter_fusion) | non-fusion elementwise | flops 9437184 | bytes 56623104 | tf_op jit(solution)/shard_map/convert_element_type | solution.py:91
  935.0 14.2 %all-reduce.9 = (bf16[256]{0:T(256)(128)(2,1)S(1)}, bf16[256]{0:T(256)(128)(2,1)S(1)}, bf16[256]{0:T(256)(128)(2,1)S(1)}) all-reduce(bf16[256]{0:T(256)(128)(2,1)S(1)} %dynamic-slice.4, bf16[256]{0:T(256)(128)(2,1)S(1)} %dynamic-slice.8, bf16[256]{0:T(256)(128)(2,1)S(1)} %dynamic-slice.12), channel_id=3, replica_groups=mesh['row'=4,'col'=8] {'col'}, use_global_device_ids=true, to_apply=%region_12.13.clone | all-reduce | flops 768 | bytes 3072
  950.4 1.5 convert_element_type.148
  951.9 1.1 copy.86
  953.0 0.8 convert_element_type.146
  953.8 1.8 convert_element_type.154
  955.5 1.8 convert_element_type.152
  (136 shorter events, 9.8 us)
Async XLA Ops:
  7.2 61.8 %copy-start.28 = (u32[32]{0:T(128)S(1)}, u32[32]{0:T(128)}, u32[]{:S(2)}) copy-start(u32[32]{0:T(128)} %constant.40) | copy-start | bytes 388
  7.2 63.0 %copy-start.29 = (bf16[32]{0:T(256)(128)(2,1)S(1)}, bf16[32]{0:T(256)(128)(2,1)}, u32[]{:S(2)}) copy-start(bf16[32]{0:T(256)(128)(2,1)} %param.15) | copy-start | bytes 196
  7.2 63.3 %copy-start.30 = (bf16[32]{0:T(256)(128)(2,1)S(1)}, bf16[32]{0:T(256)(128)(2,1)}, u32[]{:S(2)}) copy-start(bf16[32]{0:T(256)(128)(2,1)} %param.12) | copy-start | bytes 196
  7.2 63.5 %copy-start.31 = (bf16[32]{0:T(256)(128)(2,1)S(1)}, bf16[32]{0:T(256)(128)(2,1)}, u32[]{:S(2)}) copy-start(bf16[32]{0:T(256)(128)(2,1)} %param.11) | copy-start | bytes 196
  7.2 95.0 %copy-start.26 = (s32[9,128]{1,0:T(8,128)S(1)}, s32[9,128]{1,0:T(8,128)}, u32[]{:S(2)}) copy-start(s32[9,128]{1,0:T(8,128)} %param.18) | copy-start | bytes 13828
  7.2 30.4 %all-gather.11.cloned.1.call-start = ((), (), s32[]{:S(2)}) async-start(), calls=%async_computation.8 | async-start | bytes 1769472 | tf_op jit(solution)/shard_map/all_gather | solution.py:30
  8.0 60.9 %all-gather.17.cloned.1.call-start = ((), (), s32[]{:S(2)}) async-start(), calls=%async_computation.11 | async-start | bytes 2359296 | tf_op jit(solution)/shard_map/all_gather | solution.py:32
  8.7 169.6 %all-gather.21.cloned.1.call-start = ((), (), s32[]{:S(2)}) async-start(), calls=%async_computation.13 | async-start | bytes 2359296 | tf_op jit(solution)/shard_map/all_gather | solution.py:33
  9.4 169.8 %all-gather.13.cloned.1.call-start = ((), (), s32[]{:S(2)}) async-start(), calls=%async_computation.9 | async-start | bytes 7864320 | tf_op jit(solution)/shard_map/all_gather | solution.py:39
  37.7 297.0 %all-gather.15.cloned.1.call-start = ((), (), s32[]{:S(2)}) async-start(), calls=%async_computation.10 | async-start | bytes 2621440 | tf_op jit(solution)/shard_map/all_gather | solution.py:40
  54.7 290.4 %all-gather.19.cloned.1.call-start = ((), (), s32[]{:S(2)}) async-start(), calls=%async_computation.12 | async-start | bytes 10485760 | tf_op jit(solution)/shard_map/all_gather | solution.py:41
  68.9 317.0 %all-gather.23.cloned.1.call-start = ((), (), s32[]{:S(2)}) async-start(), calls=%async_computation.14 | async-start | bytes 10485760 | tf_op jit(solution)/shard_map/all_gather | solution.py:42
  102.2 77.1 %copy-start.21 = (f32[4,1,256]{2,1,0:T(1,128)}, f32[4,1,256]{2,1,0:T(1,128)S(1)}, u32[]{:S(2)}) copy-start(f32[4,1,256]{2,1,0:T(1,128)S(1)} %convert_element_type.155) | copy-start | bytes 12292
  102.3 0.6 copy-start.10
  122.5 56.8 %copy-start.4 = (bf16[1152,1024]{0,1:T(8,128)(2,1)}, bf16[1152,1024]{0,1:T(8,128)(2,1)S(1)}, u32[]{:S(2)}) copy-start(bf16[1152,1024]{0,1:T(8,128)(2,1)S(1)} %copy.57) | copy-start | bytes 7077892
  175.4 16.7 %copy-start.14 = (bf16[4,1,256]{2,1,0:T(2,128)(2,1)}, bf16[4,1,256]{2,1,0:T(2,128)(2,1)S(1)}, u32[]{:S(2)}) copy-start(bf16[4,1,256]{2,1,0:T(2,128)(2,1)S(1)} %all-gather) | copy-start | bytes 6148
  177.8 14.3 %copy-start.12 = (f32[1152]{0:T(1024)}, f32[1152]{0:T(1024)S(1)}, u32[]{:S(2)}) copy-start(f32[1152]{0:T(1024)S(1)} %convolution_reduce_fusion) | copy-start | bytes 13828
  178.4 409.1 %reduce-scatter.13.cloned.1.call-start = ((), (), s32[]{:S(2)}) async-start(), calls=%async_computation.16 | async-start | bytes 2621440 | tf_op jit(solution)/shard_map/reduce_scatter | solution.py:166
  179.3 12.8 %copy-start.17 = (f32[1152]{0:T(1024)}, f32[1152]{0:T(1024)S(1)}, u32[]{:S(2)}) copy-start(f32[1152]{0:T(1024)S(1)} %get-tuple-element.32) | copy-start | bytes 13828
  321.7 3.7 copy-start
  328.2 2.1 copy-start.1
  345.0 88.4 %copy-start.19 = (f32[1152]{0:T(1024)}, f32[1152]{0:T(1024)S(1)}, u32[]{:S(2)}) copy-start(f32[1152]{0:T(1024)S(1)} %get-tuple-element.33) | copy-start | bytes 13828
  433.4 26.0 %copy-start.23 = (f32[1152]{0:T(1024)}, f32[1152]{0:T(1024)S(1)}, u32[]{:S(2)}) copy-start(f32[1152]{0:T(1024)S(1)} %get-tuple-element.10) | copy-start | bytes 13828
  466.6 151.3 %reduce-scatter.11.cloned.1.call-start = ((), (), s32[]{:S(2)}) async-start(), calls=%async_computation.15 | async-start | bytes 7864320 | tf_op jit(solution)/shard_map/reduce_scatter | solution.py:163
  487.7 7.9 copy-start.6
  503.4 11.7 %copy-start.7 = (bf16[9,128,16,1,64]{1,4,2,0,3:T(8,128)(2,1)S(1)}, bf16[9,128,16,1,64]{1,4,2,0,3:T(8,128)(2,1)}, u32[]{:S(2)}) copy-start(bf16[9,128,16,1,64]{1,4,2,0,3:T(8,128)(2,1)} %copy.92) | copy-start | bytes 7077892
  515.2 5.8 copy-start.2
  515.2 5.8 copy-start.3
  521.0 1.7 copy-start.9
  523.5 13.3 %copy-start.5 = (bf16[1152,1024]{0,1:T(8,128)(2,1)S(1)}, bf16[1152,1024]{0,1:T(8,128)(2,1)}, u32[]{:S(2)}) copy-start(bf16[1152,1024]{0,1:T(8,128)(2,1)} %copy-done.4) | copy-start | bytes 7077892
  523.5 13.3 %copy-start.18 = (f32[1152]{0:T(1024)S(1)}, f32[1152]{0:T(1024)}, u32[]{:S(2)}) copy-start(f32[1152]{0:T(1024)} %copy-done.17) | copy-start | bytes 13828
  523.5 13.3 %copy-start.22 = (f32[4,1,256]{2,1,0:T(1,128)S(1)}, f32[4,1,256]{2,1,0:T(1,128)}, u32[]{:S(2)}) copy-start(f32[4,1,256]{2,1,0:T(1,128)} %copy-done.21) | copy-start | bytes 12292
  532.4 4.5 copy-start.8
  547.6 160.0 %reduce-scatter.21.cloned.1.call-start = ((), (), s32[]{:S(2)}) async-start(), calls=%async_computation.20 | async-start | bytes 10485760 | tf_op jit(solution)/shard_map/reduce_scatter | solution.py:172
  569.1 228.6 %reduce-scatter.17.cloned.1.call-start = ((), (), s32[]{:S(2)}) async-start(), calls=%async_computation.18 | async-start | bytes 10485760 | tf_op jit(solution)/shard_map/reduce_scatter | solution.py:169
  587.4 363.0 %reduce-scatter.15.cloned.1.call-start = ((), (), s32[]{:S(2)}) async-start(), calls=%async_computation.17 | async-start | bytes 589824 | tf_op jit(solution)/shard_map/reduce_scatter | solution.py:189
  588.0 363.9 %reduce-scatter.25.cloned.1.call-start = ((), (), s32[]{:S(2)}) async-start(), calls=%async_computation.22 | async-start | bytes 1769472
  620.6 333.2 %reduce-scatter.23.cloned.1.call-start = ((), (), s32[]{:S(2)}) async-start(), calls=%async_computation.21 | async-start | bytes 2359296 | tf_op jit(solution)/shard_map/reduce_scatter | solution.py:195
  707.6 21.4 %copy-start.32 = (u32[32]{0:T(128)S(1)}, u32[32]{0:T(128)}, u32[]{:S(2)}) copy-start(u32[32]{0:T(128)} %constant.58) | copy-start | bytes 388
  707.6 22.6 %copy-start.15 = (bf16[4,1,256]{2,1,0:T(2,128)(2,1)S(1)}, bf16[4,1,256]{2,1,0:T(2,128)(2,1)}, u32[]{:S(2)}) copy-start(bf16[4,1,256]{2,1,0:T(2,128)(2,1)} %copy-done.14) | copy-start | bytes 6148
  707.6 247.9 %reduce-scatter.19.cloned.1.call-start = ((), (), s32[]{:S(2)}) async-start(), calls=%async_computation.19 | async-start | bytes 2359296 | tf_op jit(solution)/shard_map/reduce_scatter | solution.py:192
  730.9 66.7 %copy-start.13 = (f32[1152]{0:T(1024)S(1)}, f32[1152]{0:T(1024)}, u32[]{:S(2)}) copy-start(f32[1152]{0:T(1024)} %copy-done.12) | copy-start | bytes 13828
  730.9 66.7 %copy-start.25 = (f32[1152]{0:T(1024)S(1)}, f32[1152]{0:T(1024)}, u32[]{:S(2)}) copy-start(f32[1152]{0:T(1024)} %get-tuple-element.28) | copy-start | bytes 13828
  797.7 15.1 %copy-start.16 = (f32[1152]{0:T(1024)S(1)}, f32[1152]{0:T(1024)}, u32[]{:S(2)}) copy-start(f32[1152]{0:T(1024)} %get-tuple-element.31) | copy-start | bytes 13828
  797.7 15.1 %copy-start.20 = (f32[1152]{0:T(1024)S(1)}, f32[1152]{0:T(1024)}, u32[]{:S(2)}) copy-start(f32[1152]{0:T(1024)} %copy-done.19) | copy-start | bytes 13828
  797.7 15.1 %copy-start.24 = (f32[1152]{0:T(1024)S(1)}, f32[1152]{0:T(1024)}, u32[]{:S(2)}) copy-start(f32[1152]{0:T(1024)} %copy-done.23) | copy-start | bytes 13828
  819.5 6.2 copy-start.11
  825.7 39.5 %copy-start.27 = (bf16[1024]{0:T(1024)(128)(2,1)S(1)}, bf16[1024]{0:T(1024)(128)(2,1)}, u32[]{:S(2)}) copy-start(bf16[1024]{0:T(1024)(128)(2,1)} %get-tuple-element.9) | copy-start | bytes 6148
Sparse Core Ops, SparseCore 0:
  9.7 27.9 all-gather.10
  39.2 29.5 all-gather.16
  70.5 28.3 all-gather.20
  100.6 69.6 all-gather.12
  172.0 35.1 all-gather.14
  208.9 87.6 all-gather.18
  298.4 87.4 all-gather.22
  466.8 35.1 reduce-scatter.12
  547.7 70.2 reduce-scatter.10
  621.2 86.3 reduce-scatter.20
  711.2 86.3 reduce-scatter.16
  799.8 30.9 reduce-scatter.14
  833.1 32.4 reduce-scatter.24
  867.7 33.6 reduce-scatter.22
  903.5 34.3 reduce-scatter.18
where the time goes:
time: 975 us; the launch traced here: 964 us
  waiting for transfers between devices  245 us (25%)
  matrix products  226 us (23%)
  local copies, waits for them, and re-layouts  221 us (23%)
  other arithmetic  176 us (18%)
  blocking collectives  78.4 us (8%)
  between operations  16.9 us (2%)
    reduce_scatter x1, waiting for transfers between devices, local(): lax.psum_scatter(down_part.astype(jnp.bfloat16), 'row', scatter_dimension...  86.9 us
    unnamed x86, local copies, waits for them, and re-layouts  70.9 us
    reduce_scatter x1, waiting for transfers between devices, local(): lax.psum_scatter(up_part.astype(jnp.bfloat16), 'row', scatter_dimension=0...  60.6 us
    scatter-add x1, other arithmetic, local(): input_grad = grad_out.at[token_rows].add(grad_picked)  39.5 us
    scatter-add x1, other arithmetic, local(): output = tokens.astype(jnp.float32).at[token_rows].add(gate_value[:, None...  39.4 us
    unnamed x3, blocking collectives  38.8 us
    slice x1, local copies, waits for them, and re-layouts, local(): values = heads_qkv[:, :, :, 2]  35.7 us
    reshape x1, local copies, waits for them, and re-layouts, local(): heads_qkv = projected.reshape(seq_local, routed, HEADS, 3, HD)  30.3 us
  transfers between devices with their start and end apart: 15, of which 6 were waited for; matrix products, arithmetic and copies ran while one was open for 55% of the time, Pallas kernels for 0%

commit v1 on v0

--- a/solution.py
+++ b/solution.py
@@ -6,6 +6,27 @@
 HEADS = 16
 HD = 64
 epsilon = 1e-06
+
+
+def gather_around(x, axis, dim):
+    devices, index, span = (lax.axis_size(axis), lax.axis_index(axis), x.shape[dim])
+    right = [(i, (i + 1) % devices) for i in range(devices)]
+    left = [(i, (i - 1) % devices) for i in range(devices)]
+    filled = jnp.zeros((*x.shape[:dim], devices * span, *x.shape[dim + 1 :]), x.dtype)
+    filled = lax.dynamic_update_slice_in_dim(filled, x, index * span, axis=dim)
+    from_left = from_right = x
+    half = devices // 2
+    for turn in range(1, half + 1):
+        from_left = lax.ppermute(from_left, axis, right)
+        filled = lax.dynamic_update_slice_in_dim(
+            filled, from_left, (index - turn) % devices * span, axis=dim
+        )
+        if turn < devices - half:
+            from_right = lax.ppermute(from_right, axis, left)
+            filled = lax.dynamic_update_slice_in_dim(
+                filled, from_right, (index + turn) % devices * span, axis=dim
+            )
+    return filled
 
 
 def local(
@@ -39,7 +60,7 @@
         lax.all_gather(col_pieces[0], "row", axis=0, tiled=True),
         lax.all_gather(col_pieces[1], "row", axis=1, tiled=True),
         lax.all_gather(col_pieces[2], "row", axis=0, tiled=True),
-        lax.all_gather(col_pieces[3], "row", axis=1, tiled=True),
+        gather_around(col_pieces[3], "row", 1),
         lax.all_gather(col_pieces[4], "row", axis=0, tiled=True),
         lax.all_gather(col_pieces[5], "row", axis=0, tiled=True),
         lax.all_gather(col_pieces[6], "row", axis=0, tiled=True),

time: 975 us -> 1190 us (1.22)
  blocking collectives: 78.4 us -> 203 us
  waiting for transfers between devices: 245 us -> 312 us
  local copies, waits for them, and re-layouts: 221 us -> 237 us
    all_gather x1, blocking collectives: 7.9 us -> 131 us  [local(): lax.all_gather(col_pieces[5], 'row', axis=0, tiled=True)]
    ppermute x0 -> x3, waiting for transfers between devices: none -> 61.8 us  [the longest x2 61.8 us: gather_around(): from_left = lax.ppermute(from_left, axis, right)]
    all_gather x1, waiting for transfers between devices: 0.01 us -> 29.8 us  [local(): lax.all_gather(down_weight, 'col', axis=0, tiled=True)]
    reduce_scatter x1, waiting for transfers between devices: 86.9 us -> 59.8 us  [local(): lax.psum_scatter(down_part.astype(jnp.bfloat16), 'row', scatter_dimension...]
    reduce_scatter x1, waiting for transfers between devices: 60.6 us -> 86.9 us  [local(): lax.psum_scatter(up_part.astype(jnp.bfloat16), 'row', scatter_dimension=0...]
    all_gather x1, waiting for transfers between devices: 22.6 us -> 0.01 us  [local(): lax.all_gather(back_pieces[3], 'row', axis=1, tiled=True)]
    unnamed x86 -> x88, local copies, waits for them, and re-layouts: 70.9 us -> 70.8 us
  transfers between devices with their start and end apart: 15 -> 18, of which waited for: 6 -> 7; matrix products, arithmetic and copies ran while one was open for 55% -> 47% of each run, Pallas kernels for 0% -> 0%
where the time goes in v1:
time: 1190 us; the launch traced here: 1180 us
  waiting for transfers between devices  312 us (26%)
  local copies, waits for them, and re-layouts  237 us (20%)
  matrix products  225 us (19%)
  blocking collectives  203 us (17%)
  other arithmetic  176 us (15%)
  between operations  16.9 us (1%)
    all_gather x1, blocking collectives, local(): lax.all_gather(col_pieces[5], 'row', axis=0, tiled=True)  131 us
    reduce_scatter x1, waiting for transfers between devices, local(): lax.psum_scatter(up_part.astype(jnp.bfloat16), 'row', scatter_dimension=0...  86.9 us
    unnamed x88, local copies, waits for them, and re-layouts  70.8 us
    ppermute x2, waiting for transfers between devices, gather_around(): from_left = lax.ppermute(from_left, axis, right)  61.8 us
    reduce_scatter x1, waiting for transfers between devices, local(): lax.psum_scatter(down_part.astype(jnp.bfloat16), 'row', scatter_dimension...  59.8 us
    scatter-add x1, other arithmetic, local(): input_grad = grad_out.at[token_rows].add(grad_picked)  39.5 us
    scatter-add x1, other arithmetic, local(): output = tokens.astype(jnp.float32).at[token_rows].add(gate_value[:, None...  39.3 us
    unnamed x3, blocking collectives  38.4 us
  transfers between devices with their start and end apart: 18, of which 7 were waited for; matrix products, arithmetic and copies ran while one was open for 47% of the time, Pallas kernels for 0%

profile of v1, /device:TPU:0, one launch (start us, length us, event | category | flops | bytes accessed | tf_op | source)
XLA Modules:
  0.0 1175.6 jit_solution(9891298022457914160)
XLA Ops:
  9.5 28.1 %all-gather.11.cloned.1.call-done = bf16[256,3072]{1,0:T(8,128)(2,1)} async-done(((bf16[256,384]{1,0:T(8,128)(2,1)}), bf16[256,3072]{1,0:T(8,128)(2,1)}) %all-gather.11.cloned.1.call-update) | async-done | bytes 1572880 | tf_op jit(solution)/shard_map/all_gather | solution.py:51
  37.7 16.9 %all_gather.55 = bf16[1024,256]{1,0:T(8,128)(2,1)} all-gather(bf16[128,256]{1,0:T(8,128)(2,1)} %param.14), channel_id=1, replica_groups=mesh['row'=4,'col'=8] {'col'}, dimensions={0}, use_global_device_ids=true | all-gather | bytes 589824 | tf_op jit(solution)/shard_map/all_gather | solution.py:52
  54.7 14.2 %all-gather.17.cloned.1.call-done = bf16[256,4096]{1,0:T(8,128)(2,1)} async-done(((bf16[256,512]{1,0:T(8,128)(2,1)}), bf16[256,4096]{1,0:T(8,128)(2,1)}) %all-gather.17.cloned.1.call-update) | async-done | bytes 2097168 | tf_op jit(solution)/shard_map/all_gather | solution.py:53
  68.9 29.8 %all-gather.21.cloned.1.call-done = bf16[4096,256]{1,0:T(8,128)(2,1)} async-done(((bf16[512,256]{1,0:T(8,128)(2,1)}), bf16[4096,256]{1,0:T(8,128)(2,1)}) %all-gather.21.cloned.1.call-update) | async-done | bytes 2097168 | tf_op jit(solution)/shard_map/all_gather | solution.py:54
  103.9 14.8 %all-reduce.10 = (bf16[256]{0:T(256)(128)(2,1)S(1)}, bf16[256]{0:T(256)(128)(2,1)S(1)}, bf16[256]{0:T(256)(128)(2,1)S(1)}) all-reduce(bf16[256]{0:T(256)(128)(2,1)S(1)} %dynamic-update-slice.1, bf16[256]{0:T(256)(128)(2,1)S(1)} %dynamic-update-slice.2, bf16[256]{0:T(256)(128)(2,1)S(1)} %dynamic-update-slice), channel_id=1, replica_groups=mesh['row'=4,'col'=8] {'col'}, use_global_device_ids=true, to_apply=%add.1 | all-reduce | flops 768 | bytes 3072
  118.8 131.4 %all-gather.2 = bf16[4,1,256]{2,1,0:T(2,128)(2,1)S(1)} all-gather(bf16[1,1,256]{2,1,0:T(2,128)(2,1)S(1)} %reshape.157), channel_id=1, replica_groups=mesh['row'=4,'col'=8] {'row'}, dimensions={0}, use_global_device_ids=true | all-gather | bytes 2560 | tf_op jit(solution)/shard_map/all_gather | solution.py:65
  250.2 8.8 all-gather.1
  259.1 15.4 %gather_fusion = bf16[1152,1024]{1,0:T(8,128)(2,1)} fusion(bf16[9216,1024]{1,0:T(8,128)(2,1)} %param.10, s32[2048]{0:T(1024)S(1)} %pad_clamp_fusion), kind=kCustom, calls=%fused_computation | custom fusion | bytes 4723200 | tf_op jit(solution)/shard_map/gather | solution.py:72
  274.5 3.3 copy.57
  277.8 21.7 %convert_element_type.133 = f32[9216,1024]{1,0:T(8,128)} convert(bf16[9216,1024]{1,0:T(8,128)(2,1)} %param.19) | non-fusion elementwise | flops 9437184 | bytes 56623104 | tf_op jit(solution)/shard_map/convert_element_type | solution.py:126
  299.5 19.7 %gather_fusion.1 = f32[1152,1024]{1,0:T(8,128)} fusion(f32[9216,1024]{1,0:T(8,128)} %convert_element_type.133, s32[2048]{0:T(1024)S(1)} %pad_clamp_fusion), kind=kCustom, calls=%fused_computation.1 | custom fusion | bytes 9441792 | tf_op jit(solution)/shard_map/gather | solution.py:127
  319.2 6.1 copy.65
  325.3 7.3 all-gather
  332.7 2.4 convolution_reduce_fusion
  338.4 4.3 broadcast_in_dim.14
  344.2 3.1 constant_dynamic-update-slice_fusion.2
  347.3 3.2 constant_dynamic-update-slice_fusion.1
  350.5 61.8 %collective-permute-done.2 = bf16[4096,256]{1,0:T(8,128)(2,1)} collective-permute-done((bf16[4096,256]{1,0:T(8,128)(2,1)}, bf16[4096,256]{1,0:T(8,128)(2,1)}, u32[]{:S(2)}, u32[]{:S(2)}) %collective-permute-start.2) | collective-permute-done | bytes 2097184 | tf_op jit(solution)/shard_map/ppermute | solution.py:20
  412.3 3.1 constant_dynamic-update-slice_fusion
  415.4 12.8 %convolution_convert_fusion = bf16[1152,3072]{1,0:T(8,128)(2,1)} fusion(bf16[1024,3072]{1,0:T(8,128)(2,1)} %all-gather.13.cloned.1.call-done, bf16[1152,1024]{0,1:T(8,128)(2,1)S(1)} %copy.57, f32[1024]{0:T(1024)S(1)} %bitcast.115, f32[1152]{0:T(1024)S(1)} %get-tuple-element.32), kind=kOutput, calls=%fused_computation.21 | convolution fusion | flops 7256014848 | bytes 15737344 | tf_op jit(solution)/shard_map/dot_general | solution.py:79
  428.2 30.2 %reshape.178 = bf16[9,128,16,3,64]{4,3,2,1,0:T(4,128)(2,1)} reshape(bf16[1152,3072]{1,0:T(8,128)(2,1)} %convolution_convert_fusion) | data formatting | bytes 14155776 | tf_op jit(solution)/shard_map/reshape | solution.py:80
  458.5 35.7 %fusion.63 = (bf16[9,128,16,1,64]{4,3,2,1,0:T(2,128)(2,1)}, bf16[9,128,16,1,64]{4,3,2,1,0:T(2,128)(2,1)}, bf16[9,128,16,1,64]{4,3,2,1,0:T(2,128)(2,1)}) fusion(bf16[9,128,16,3,64]{4,3,2,1,0:T(4,128)(2,1)} %reshape.178), kind=kLoop, calls=%fused_computation.110 | loop fusion | bytes 14155776 | tf_op jit(solution)/shard_map/slice | solution.py:83
  494.2 18.9 %copy.91 = bf16[9,128,16,1,64]{1,4,2,0,3:T(8,128)(2,1)S(1)} copy(bf16[9,128,16,1,64]{4,3,2,1,0:T(2,128)(2,1)} %get-tuple-element.25) | data formatting | bytes 4718592
  513.0 20.0 %copy.92 = bf16[9,128,16,1,64]{1,4,2,0,3:T(8,128)(2,1)} copy(bf16[9,128,16,1,64]{4,3,2,1,0:T(2,128)(2,1)} %get-tuple-element.26) | data formatting | bytes 4718592
  533.0 20.0 %copy.93 = bf16[9,128,16,1,64]{1,4,2,0,3:T(8,128)(2,1)} copy(bf16[9,128,16,1,64]{4,3,2,1,0:T(2,128)(2,1)} %get-tuple-element.27) | data formatting | bytes 4718592
  553.1 4.5 fusion.15
  557.6 3.1 fusion.7
  561.2 2.8 divide_convert_fusion
  564.0 2.0 convert_bitcast_fusion.1
  566.1 4.4 copy.63
  570.6 10.1 multiply_reduce_fusion.4
  580.8 17.8 %fusion.62 = f32[1152,4096]{1,0:T(8,128)} fusion(bf16[1024,4096]{1,0:T(8,128)(2,1)} %all-gather.19.cloned.1.call-done, f32[1152,1024]{0,1:T(8,128)} %get-tuple-element.24, f32[1024]{0:T(1024)S(1)} %bitcast.110, f32[1152]{0:T(1024)S(1)} %get-tuple-element.34), kind=kOutput, calls=%fused_computation.109 | convolution fusion | flops 9667215360 | bytes 31990272 | tf_op jit(solution)/shard_map/dot_general | solution.py:103
  598.6 28.2 %fusion.6 = bf16[1152,4096]{1,0:T(8,128)(2,1)} fusion(f32[1152,4096]{1,0:T(8,128)} %fusion.62, bf16[4096,1024]{1,0:T(8,128)(2,1)} %all-gather.23.cloned.1.call-done, f32[1152,1024]{0,1:T(8,128)} %copy.65, f32[1152]{0:T(1024)S(1)} %add_divide_fusion), kind=kOutput, calls=%fused_computation.12 | convolution fusion | flops 9760407552 | bytes 41423360 | tf_op jit(solution)/shard_map/dot_general | solution.py:131
  626.8 19.3 %multiply_reduce_fusion.1 = (bf16[1024]{0:T(1024)(128)(2,1)}, f32[1152]{0:T(1024)S(1)}, f32[1152,1024]{0,1:T(8,128)}) fusion(f32[1152,1024]{0,1:T(8,128)} %get-tuple-element.24, f32[1152]{0:T(1024)S(1)} %get-tuple-element.34, f32[1024]{0:T(1024)S(1)} %bitcast.111, bf16[1152,4096]{1,0:T(8,128)(2,1)} %fusion.6, ...), kind=kOutput, calls=%fused_computation.50 | convolution fusion | flops 9670752256 | bytes 27278336 | tf_op jit(solution)/shard_map/dot_general | solution.py:135
  646.1 25.9 %multiply_reduce_fusion.2 = (f32[1152]{0:T(1024)}, f32[1152,1024]{0,1:T(8,128)}, bf16[1152,1024]{0,1:T(8,128)(2,1)}) fusion(f32[1152,1024]{0,1:T(8,128)} %copy.65, f32[1152]{0:T(1024)S(1)} %add_divide_fusion, f32[1152]{0:T(1024)S(1)} %get-tuple-element.10, f32[1152,1024]{0,1:T(8,128)} %get-tuple-element.24, f32[1152]{0:T(1024)S(1)} %get-tuple-element.33, ...), kind=kOutput, calls=%fused_computation.51 | convolution fusion | flops 9721478144 | bytes 53242368 | tf_op jit(solution)/shard_map/dot_general | solution.py:106
  672.1 7.2 fusion.53
  679.3 6.4 convolution_convert_fusion.3
  685.7 7.7 reshape.179
  693.4 7.0 copy.68
  700.4 7.9 convert_bitcast_fusion
  708.3 7.7 multiply_reduce_fusion
  716.1 11.8 %multiply_convert_fusion.1 = bf16[9,16,128,128]{2,3,1,0:T(8,128)(2,1)} fusion(f32[9,16,128,128]{2,3,1,0:T(8,128)} %get-tuple-element.42, f32[9,16,128,128]{2,3,1,0:T(8,128)} %copy-done, f32[9,16,128]{2,1,0:T(8,128)S(1)} %get-tuple-element.41, f32[9,16,128]{2,1,0:T(8,128)S(1)} %log_add_fusion, pred[128,128]{0,1:T(8,128)(4,1)S(1)} %iota_compare_fusion), kind=kLoop, calls=%fused_computation.22 | loop fusion | flops 14155776 | bytes 23756800 | tf_op jit(solution)/shard_map/convert_element_type | solution.py:156
  727.9 5.8 fusion.31
  736.2 8.8 copy.73
  745.1 4.5 copy-done.8
  749.6 10.8 fusion.12
  760.4 17.9 %convolution_convert_fusion.2 = bf16[1024,4096]{1,0:T(8,128)(2,1)} fusion(bf16[1152,4096]{1,0:T(8,128)(2,1)} %fusion.6, f32[1152,1024]{0,1:T(8,128)} %get-tuple-element.24, f32[1024]{0:T(1024)S(1)} %bitcast.113, f32[1152]{0:T(1024)S(1)} %get-tuple-element.34), kind=kOutput, calls=%fused_computation.30 | convolution fusion | flops 9671409664 | bytes 22553088 | tf_op jit(solution)/shard_map/dot_general | solution.py:134
  778.4 21.9 %convolution_convert_fusion.1 = bf16[4096,1024]{1,0:T(8,128)(2,1)} fusion(f32[1152,1024]{0,1:T(8,128)} %copy.65, f32[1152]{0:T(1024)S(1)} %add_divide_fusion, f32[1152,4096]{1,0:T(8,128)} %fusion.62), kind=kOutput, calls=%fused_computation.29 | convolution fusion | flops 9712697344 | bytes 31986176 | tf_op jit(solution)/shard_map/dot_general | solution.py:132
  801.0 28.8 %reduce-scatter.11.cloned.1.call-done = bf16[256,3072]{1,0:T(8,128)(2,1)} async-done(((bf16[1024,3072]{1,0:T(8,128)(2,1)}), bf16[256,3072]{1,0:T(8,128)(2,1)}) %reduce-scatter.11.cloned.1.call-update) | async-done | bytes 1572880 | tf_op jit(solution)/shard_map/reduce_scatter | solution.py:184
  829.8 2.6 copy.85
  832.5 86.9 %reduce-scatter.17.cloned.1.call-done = bf16[256,4096]{1,0:T(8,128)(2,1)} async-done(((bf16[1024,4096]{1,0:T(8,128)(2,1)}), bf16[256,4096]{1,0:T(8,128)(2,1)}) %reduce-scatter.17.cloned.1.call-update) | async-done | bytes 2097168 | tf_op jit(solution)/shard_map/reduce_scatter | solution.py:190
  919.5 21.4 %convert_element_type.120 = f32[9216,1024]{1,0:T(8,128)} convert(bf16[9216,1024]{1,0:T(8,128)(2,1)} %param.10) | non-fusion elementwise | flops 9437184 | bytes 56623104 | tf_op jit(solution)/shard_map/convert_element_type | solution.py:109
  942.8 6.2 copy.64
  949.0 59.8 %reduce-scatter.21.cloned.1.call-done = bf16[4096,256]{1,0:T(8,128)(2,1)} async-done(((bf16[4096,1024]{1,0:T(8,128)(2,1)}), bf16[4096,256]{1,0:T(8,128)(2,1)}) %reduce-scatter.21.cloned.1.call-update) | async-done | bytes 2097168 | tf_op jit(solution)/shard_map/reduce_scatter | solution.py:193
  1008.9 15.1 %fusion.27 = (bf16[1024]{0:T(1024)(128)(2,1)S(1)}, f32[1152]{0:T(1024)S(1)}, bf16[1024]{0:T(1024)(128)(2,1)S(1)}, f32[1152,1024]{0,1:T(8,128)S(1)}) fusion(bf16[1152,1024]{0,1:T(8,128)(2,1)S(1)} %copy-done.5, f32[1152]{0:T(1024)S(1)} %copy-done.19, f32[1024]{0:T(1024)S(1)} %bitcast.117, f32[1152]{0:T(1024)S(1)} %subtract_multiply_fusion, ...), kind=kOutput, calls=%fused_computation.49 | convolution fusion | flops 7258371072 | bytes 20469248 | tf_op jit(solution)/shard_map/dot_general | solution.py:174
  1024.0 6.8 fusion.23
  1030.8 6.1 copy.76
  1036.9 39.5 %scatter_fusion.1 = f32[9216,1024]{1,0:T(8,128)} fusion(f32[9216,1024]{1,0:T(8,128)} %convert_element_type.133, s32[1152]{0:T(1024)S(1)} %copy-done.12, f32[1152,1024]{1,0:T(8,128)} %copy.76), kind=kCustom, calls=%fused_computation.3 | custom fusion | flops 1179648 | bytes 14160384 | tf_op jit(solution)/shard_map/scatter-add | solution.py:182
  1076.4 9.4 all-reduce.11
  1086.0 39.3 %scatter_fusion = f32[9216,1024]{1,0:T(8,128)} fusion(f32[9216,1024]{1,0:T(8,128)} %convert_element_type.120, s32[1152]{0:T(1024)S(1)} %copy-done.12, f32[1152,1024]{1,0:T(8,128)} %copy.64), kind=kCustom, calls=%fused_computation.2 | custom fusion | flops 1179648 | bytes 14160384 | tf_op jit(solution)/shard_map/scatter-add | solution.py:111
  1125.3 20.9 %convert_element_type.132 = bf16[9216,1024]{1,0:T(8,128)(2,1)} convert(f32[9216,1024]{1,0:T(8,128)} %scatter_fusion) | non-fusion elementwise | flops 9437184 | bytes 56623104 | tf_op jit(solution)/shard_map/convert_element_type | solution.py:112
  1146.2 14.2 %all-reduce.9 = (bf16[256]{0:T(256)(128)(2,1)S(1)}, bf16[256]{0:T(256)(128)(2,1)S(1)}, bf16[256]{0:T(256)(128)(2,1)S(1)}) all-reduce(bf16[256]{0:T(256)(128)(2,1)S(1)} %dynamic-slice.4, bf16[256]{0:T(256)(128)(2,1)S(1)} %dynamic-slice.8, bf16[256]{0:T(256)(128)(2,1)S(1)} %dynamic-slice.12), channel_id=3, replica_groups=mesh['row'=4,'col'=8] {'col'}, use_global_device_ids=true, to_apply=%region_12.13.clone | all-reduce | flops 768 | bytes 3072
  1165.0 1.8 convert_element_type.152
  1166.8 1.8 convert_element_type.154
  (149 shorter events, 21.2 us)
Async XLA Ops:
  7.2 94.8 %copy-start.29 = (u32[32]{0:T(128)S(1)}, u32[32]{0:T(128)}, u32[]{:S(2)}) copy-start(u32[32]{0:T(128)} %constant.78) | copy-start | bytes 388
  7.2 93.0 %copy-start.27 = (s32[9,128]{1,0:T(8,128)S(1)}, s32[9,128]{1,0:T(8,128)}, u32[]{:S(2)}) copy-start(s32[9,128]{1,0:T(8,128)} %param.18) | copy-start | bytes 13828
  7.2 96.0 %copy-start.30 = (bf16[32]{0:T(256)(128)(2,1)S(1)}, bf16[32]{0:T(256)(128)(2,1)}, u32[]{:S(2)}) copy-start(bf16[32]{0:T(256)(128)(2,1)} %param.15) | copy-start | bytes 196
  7.2 96.2 %copy-start.31 = (bf16[32]{0:T(256)(128)(2,1)S(1)}, bf16[32]{0:T(256)(128)(2,1)}, u32[]{:S(2)}) copy-start(bf16[32]{0:T(256)(128)(2,1)} %param.12) | copy-start | bytes 196
  7.2 96.5 %copy-start.32 = (bf16[32]{0:T(256)(128)(2,1)S(1)}, bf16[32]{0:T(256)(128)(2,1)}, u32[]{:S(2)}) copy-start(bf16[32]{0:T(256)(128)(2,1)} %param.11) | copy-start | bytes 196
  7.2 30.4 %all-gather.11.cloned.1.call-start = ((), (), s32[]{:S(2)}) async-start(), calls=%async_computation.8 | async-start | bytes 1769472 | tf_op jit(solution)/shard_map/all_gather | solution.py:51
  8.0 60.9 %all-gather.17.cloned.1.call-start = ((), (), s32[]{:S(2)}) async-start(), calls=%async_computation.11 | async-start | bytes 2359296 | tf_op jit(solution)/shard_map/all_gather | solution.py:53
  8.7 90.0 %all-gather.21.cloned.1.call-start = ((), (), s32[]{:S(2)}) async-start(), calls=%async_computation.13 | async-start | bytes 2359296 | tf_op jit(solution)/shard_map/all_gather | solution.py:54
  9.4 406.0 %all-gather.13.cloned.1.call-start = ((), (), s32[]{:S(2)}) async-start(), calls=%async_computation.9 | async-start | bytes 7864320 | tf_op jit(solution)/shard_map/all_gather | solution.py:60
  37.7 532.9 %all-gather.15.cloned.1.call-start = ((), (), s32[]{:S(2)}) async-start(), calls=%async_computation.10 | async-start | bytes 2621440 | tf_op jit(solution)/shard_map/all_gather | solution.py:61
  54.7 526.1 %all-gather.19.cloned.1.call-start = ((), (), s32[]{:S(2)}) async-start(), calls=%async_computation.12 | async-start | bytes 10485760 | tf_op jit(solution)/shard_map/all_gather | solution.py:62
  68.9 529.7 %all-gather.23.cloned.1.call-start = ((), (), s32[]{:S(2)}) async-start(), calls=%async_computation.14 | async-start | bytes 10485760 | tf_op jit(solution)/shard_map/all_gather | solution.py:124
  98.8 236.4 %collective-permute-start = (bf16[4096,256]{1,0:T(8,128)(2,1)}, bf16[4096,256]{1,0:T(8,128)(2,1)}, u32[]{:S(2)}, u32[]{:S(2)}) collective-permute-start(bf16[4096,256]{1,0:T(8,128)(2,1)} %all-gather.21.cloned.1.call-done), channel_id=1, source_target_pairs={{0,8},{8,16},{16,24},{24,0},{1,9},{9,17},{17,25},{25,1},{2,10},{10... | collective-permute-start | bytes 6291464 | tf_op jit(solution)/shard_map/ppermute | solution.py:20
  100.3 1.5 copy-start.11
  100.3 247.0 %collective-permute-start.1 = (bf16[4096,256]{1,0:T(8,128)(2,1)}, bf16[4096,256]{1,0:T(8,128)(2,1)}, u32[]{:S(2)}, u32[]{:S(2)}) collective-permute-start(bf16[4096,256]{1,0:T(8,128)(2,1)} %all-gather.21.cloned.1.call-done), channel_id=1, source_target_pairs={{0,24},{8,0},{16,8},{24,16},{1,25},{9,1},{17,9},{25,17},{2,26},{10... | collective-permute-start | bytes 6291464 | tf_op jit(solution)/shard_map/ppermute | solution.py:25
  259.1 156.4 %copy-start.22 = (f32[4,1,256]{2,1,0:T(1,128)}, f32[4,1,256]{2,1,0:T(1,128)S(1)}, u32[]{:S(2)}) copy-start(f32[4,1,256]{2,1,0:T(1,128)S(1)} %convert_element_type.155) | copy-start | bytes 12292
  277.7 137.7 %copy-start.4 = (bf16[1152,1024]{0,1:T(8,128)(2,1)}, bf16[1152,1024]{0,1:T(8,128)(2,1)S(1)}, u32[]{:S(2)}) copy-start(bf16[1152,1024]{0,1:T(8,128)(2,1)S(1)} %copy.57) | copy-start | bytes 7077892
  332.7 4.5 copy-start.15
  335.1 0.6 copy-start.13
  335.7 76.6 %collective-permute-start.2 = (bf16[4096,256]{1,0:T(8,128)(2,1)}, bf16[4096,256]{1,0:T(8,128)(2,1)}, u32[]{:S(2)}, u32[]{:S(2)}) collective-permute-start(bf16[4096,256]{1,0:T(8,128)(2,1)} %collective-permute-done), channel_id=1, source_target_pairs={{0,8},{8,16},{16,24},{24,0},{1,9},{9,17},{17,25},{25,1},{2,10},{10... | collective-permute-start | bytes 6291464 | tf_op jit(solution)/shard_map/ppermute | solution.py:20
  338.3 77.1 %copy-start.18 = (f32[1152]{0:T(1024)}, f32[1152]{0:T(1024)S(1)}, u32[]{:S(2)}) copy-start(f32[1152]{0:T(1024)S(1)} %get-tuple-element.32) | copy-start | bytes 13828
  338.4 462.1 %reduce-scatter.13.cloned.1.call-start = ((), (), s32[]{:S(2)}) async-start(), calls=%async_computation.16 | async-start | bytes 2621440 | tf_op jit(solution)/shard_map/reduce_scatter | solution.py:187
  338.4 4.3 copy-start.10
  557.5 3.6 copy-start
  564.0 2.1 copy-start.1
  580.7 65.4 %copy-start.20 = (f32[1152]{0:T(1024)}, f32[1152]{0:T(1024)S(1)}, u32[]{:S(2)}) copy-start(f32[1152]{0:T(1024)S(1)} %get-tuple-element.33) | copy-start | bytes 13828
  646.1 25.9 %copy-start.24 = (f32[1152]{0:T(1024)}, f32[1152]{0:T(1024)S(1)}, u32[]{:S(2)}) copy-start(f32[1152]{0:T(1024)S(1)} %get-tuple-element.10) | copy-start | bytes 13828
  679.2 150.5 %reduce-scatter.11.cloned.1.call-start = ((), (), s32[]{:S(2)}) async-start(), calls=%async_computation.15 | async-start | bytes 7864320 | tf_op jit(solution)/shard_map/reduce_scatter | solution.py:184
  700.4 7.9 copy-start.6
  716.1 11.8 %copy-start.7 = (bf16[9,128,16,1,64]{1,4,2,0,3:T(8,128)(2,1)S(1)}, bf16[9,128,16,1,64]{1,4,2,0,3:T(8,128)(2,1)}, u32[]{:S(2)}) copy-start(bf16[9,128,16,1,64]{1,4,2,0,3:T(8,128)(2,1)} %copy.92) | copy-start | bytes 7077892
  727.9 5.8 copy-start.2
  727.9 5.8 copy-start.3
  733.7 1.7 copy-start.9
  736.2 13.4 %copy-start.5 = (bf16[1152,1024]{0,1:T(8,128)(2,1)S(1)}, bf16[1152,1024]{0,1:T(8,128)(2,1)}, u32[]{:S(2)}) copy-start(bf16[1152,1024]{0,1:T(8,128)(2,1)} %copy-done.4) | copy-start | bytes 7077892
  736.2 13.4 %copy-start.19 = (f32[1152]{0:T(1024)S(1)}, f32[1152]{0:T(1024)}, u32[]{:S(2)}) copy-start(f32[1152]{0:T(1024)} %copy-done.18) | copy-start | bytes 13828
  736.2 13.4 %copy-start.23 = (f32[4,1,256]{2,1,0:T(1,128)S(1)}, f32[4,1,256]{2,1,0:T(1,128)}, u32[]{:S(2)}) copy-start(f32[4,1,256]{2,1,0:T(1,128)} %copy-done.22) | copy-start | bytes 12292
  745.0 4.5 copy-start.8
  760.4 159.0 %reduce-scatter.17.cloned.1.call-start = ((), (), s32[]{:S(2)}) async-start(), calls=%async_computation.18 | async-start | bytes 10485760 | tf_op jit(solution)/shard_map/reduce_scatter | solution.py:190
  778.4 230.4 %reduce-scatter.21.cloned.1.call-start = ((), (), s32[]{:S(2)}) async-start(), calls=%async_computation.20 | async-start | bytes 10485760 | tf_op jit(solution)/shard_map/reduce_scatter | solution.py:193
  800.4 361.3 %reduce-scatter.15.cloned.1.call-start = ((), (), s32[]{:S(2)}) async-start(), calls=%async_computation.17 | async-start | bytes 589824 | tf_op jit(solution)/shard_map/reduce_scatter | solution.py:210
  801.0 362.2 %reduce-scatter.25.cloned.1.call-start = ((), (), s32[]{:S(2)}) async-start(), calls=%async_computation.22 | async-start | bytes 1769472
  832.4 332.6 %reduce-scatter.19.cloned.1.call-start = ((), (), s32[]{:S(2)}) async-start(), calls=%async_computation.19 | async-start | bytes 2359296 | tf_op jit(solution)/shard_map/reduce_scatter | solution.py:213
  919.4 21.4 %copy-start.33 = (u32[32]{0:T(128)S(1)}, u32[32]{0:T(128)}, u32[]{:S(2)}) copy-start(u32[32]{0:T(128)} %constant.96) | copy-start | bytes 388
  919.4 22.7 %copy-start.16 = (bf16[4,1,256]{2,1,0:T(2,128)(2,1)S(1)}, bf16[4,1,256]{2,1,0:T(2,128)(2,1)}, u32[]{:S(2)}) copy-start(bf16[4,1,256]{2,1,0:T(2,128)(2,1)} %copy-done.15) | copy-start | bytes 6148
  919.4 247.4 %reduce-scatter.23.cloned.1.call-start = ((), (), s32[]{:S(2)}) async-start(), calls=%async_computation.21 | async-start | bytes 2359296 | tf_op jit(solution)/shard_map/reduce_scatter | solution.py:216
  942.8 66.1 %copy-start.14 = (f32[1152]{0:T(1024)S(1)}, f32[1152]{0:T(1024)}, u32[]{:S(2)}) copy-start(f32[1152]{0:T(1024)} %copy-done.13) | copy-start | bytes 13828
  942.8 66.1 %copy-start.26 = (f32[1152]{0:T(1024)S(1)}, f32[1152]{0:T(1024)}, u32[]{:S(2)}) copy-start(f32[1152]{0:T(1024)} %get-tuple-element.28) | copy-start | bytes 13828
  1008.9 15.1 %copy-start.17 = (f32[1152]{0:T(1024)S(1)}, f32[1152]{0:T(1024)}, u32[]{:S(2)}) copy-start(f32[1152]{0:T(1024)} %get-tuple-element.31) | copy-start | bytes 13828
  1008.9 15.1 %copy-start.21 = (f32[1152]{0:T(1024)S(1)}, f32[1152]{0:T(1024)}, u32[]{:S(2)}) copy-start(f32[1152]{0:T(1024)} %copy-done.20) | copy-start | bytes 13828
  1008.9 15.1 %copy-start.25 = (f32[1152]{0:T(1024)S(1)}, f32[1152]{0:T(1024)}, u32[]{:S(2)}) copy-start(f32[1152]{0:T(1024)} %copy-done.24) | copy-start | bytes 13828
  1030.8 6.1 copy-start.12
  1036.9 39.5 %copy-start.28 = (bf16[1024]{0:T(1024)(128)(2,1)S(1)}, bf16[1024]{0:T(1024)(128)(2,1)}, u32[]{:S(2)}) copy-start(bf16[1024]{0:T(1024)(128)(2,1)} %get-tuple-element.9) | copy-start | bytes 6148
Sparse Core Ops, SparseCore 0:
  9.7 27.9 all-gather.10
  39.2 29.5 all-gather.16
  70.5 28.2 all-gather.20
  100.5 120.1 all-gather.12
  222.3 42.9 all-gather.14
  267.0 106.1 all-gather.18
  375.0 99.4 all-gather.22
  679.4 34.3 reduce-scatter.12
  760.5 69.2 reduce-scatter.10
  833.0 86.3 reduce-scatter.16
  922.5 86.3 reduce-scatter.20
  1011.0 30.8 reduce-scatter.14
  1044.2 32.4 reduce-scatter.24
  1078.9 33.7 reduce-scatter.18
  1114.8 34.5 reduce-scatter.22
